TPU v7x, 256 devices: a whole 4x4x8 slice. The times are simulated.
256 devices in a mesh: row: 8 (over y, core), col: 8 (over x, z_hi), rep: 4 (over z_lo).
Axes of the slice: x: 4, y: 4, z: 8 (z_hi: 2, z_lo: 4; z = z_hi * 4 + z_lo), core: 2. Of those that a mesh axis runs over, the one named last changes fastest.
Arguments:
- features: float32 [256, 32768], P('rep', ('col', 'row')), may hold values from -6 to 6
- weight: float32 [256, 256], replicated, may hold values from -0.375 to 0.375
- cotangent: float32 [256, 32768], P('rep', ('row', 'col')), may hold values from -6 to 6
- tile_values: float32 [10240, 128, 128], P(('row', 'col')), may hold values from -0.078125 to 0.078125
- tile_row: int32 [10240], P(('row', 'col')), may hold values from 0 to 31
- tile_col: int32 [10240], P(('row', 'col')), may hold values from 0 to 31
- tile_kind: int32 [10240], P(('row', 'col')), may hold values from 0 to 159
- tile_count: int32 [64], P(('row', 'col')), may hold values from 40 to 160, as said below
Outputs:
- output: float32 [256, 32768], P('rep', ('row', 'col'))
- input_grad: float32 [256, 32768], P('rep', ('col', 'row'))
- weight_grad: float32 [256, 256], P('rep')
Inputs may be any that keep to these rules, and one draw needn't show every extreme that they name: `tile_count`: a block's slots at or after its count are not part of the adjacency; some block uses all 160 slots. `tile_row`: slots may repeat a tile position; their tiles add. `tile_kind`: an index into the 160 stored tiles of the same block.
All inputs are finite; a program needn't handle non-finite values.
Results may differ from a plain program's by a relative error of at most 0.0001.
Values sent between devices are 32-bit elements; how exact they have to be, the bound alone decides.
No kernel may reach another device: no remote copies, remote signals or barrier semaphores. Data moves between devices by JAX's collectives and lax.ppermute only.
A program may use at most 128 MiB of HBM per device.

v0:
```python
import jax
import jax.numpy as jnp
from jax import lax
from jax.sharding import PartitionSpec as P


def tile_terms(source, values, from_tile, to_tile, tile_kinds, live_weight, dest_tiles, transposed):
    feat_width = source.shape[0]
    tile_edge = values.shape[1]
    tiled = source.reshape(feat_width, source.shape[1] // tile_edge, tile_edge)
    picked = jnp.take(tiled, from_tile, axis=1)
    chosen = jnp.take(values, tile_kinds, axis=0)
    if transposed:
        products = jnp.einsum("fga,gab->fgb", picked, chosen, precision=lax.Precision.HIGHEST)
    else:
        products = jnp.einsum("fgb,gab->fga", picked, chosen, precision=lax.Precision.HIGHEST)
    onehot = (to_tile[:, None] == jnp.arange(dest_tiles, dtype=jnp.int32)[None, :]).astype(
        jnp.float32
    )
    onehot = onehot * live_weight[:, None]
    spread = jnp.einsum("fgt,gd->fdt", products, onehot, precision=lax.Precision.HIGHEST)
    return spread.reshape(feat_width, dest_tiles * tile_edge)


def aggregate(source, values, from_tile, to_tile, tile_kinds, live_count, dest_tiles, transposed):
    slot_total = tile_kinds.shape[0]
    live_weight = (jnp.arange(slot_total, dtype=jnp.int32) < live_count).astype(jnp.float32)
    return tile_terms(
        source, values, from_tile, to_tile, tile_kinds, live_weight, dest_tiles, transposed
    )


def local(features, weight, cotangent, tile_values, tile_row, tile_col, tile_kind, tile_count):
    n_rowdev = lax.axis_size("row")
    n_coldev = lax.axis_size("col")
    n_repdev = lax.axis_size("rep")
    quarter = weight.shape[0] // n_repdev
    rep_index = lax.axis_index("rep")
    own_rows = lax.dynamic_slice_in_dim(weight, rep_index * quarter, quarter, 0)
    own_cols = lax.dynamic_slice_in_dim(weight, rep_index * quarter, quarter, 1)
    stretch_len = features.shape[1]
    tile_edge = tile_values.shape[1]
    live_count = tile_count[0]
    row_tiles = n_coldev * stretch_len // tile_edge
    col_tiles = n_rowdev * stretch_len // tile_edge
    mixed = lax.psum_scatter(
        lax.dot_general(
            own_rows,
            features,
            (((0,), (0,)), ((), ())),
            precision=lax.Precision.HIGHEST,
            preferred_element_type=jnp.float32,
        ),
        "rep",
        scatter_dimension=0,
        tiled=True,
    )
    column_block = lax.all_gather(mixed, "row", axis=1, tiled=True)
    partial_value = aggregate(
        column_block, tile_values, tile_col, tile_row, tile_kind, live_count, row_tiles, False
    )
    summed = lax.psum_scatter(partial_value, "col", scatter_dimension=1, tiled=True)
    output, pullback = jax.vjp(lambda v: jax.nn.gelu(v, approximate=True), summed)
    (grad_pre,) = pullback(cotangent)
    row_block = lax.all_gather(grad_pre, "col", axis=1, tiled=True)
    partial_back = aggregate(
        row_block, tile_values, tile_row, tile_col, tile_kind, live_count, col_tiles, True
    )
    grad_mixed = lax.psum_scatter(partial_back, "row", scatter_dimension=1, tiled=True)
    input_grad = lax.psum_scatter(
        jnp.dot(
            own_cols,
            grad_mixed,
            preferred_element_type=jnp.float32,
            precision=lax.Precision.HIGHEST,
        ),
        "rep",
        scatter_dimension=0,
        tiled=True,
    )
    weight_part = lax.dot_general(
        features,
        lax.all_gather(grad_mixed, "rep", axis=0, tiled=True),
        (((1,), (1,)), ((), ())),
        precision=lax.Precision.HIGHEST,
        preferred_element_type=jnp.float32,
    )
    node_total = stretch_len * n_rowdev * n_coldev
    weight_grad = lax.psum(weight_part * float(node_total) ** (-0.5), ("row", "col"))
    return (output, input_grad, weight_grad)


def solution(mesh):
    return jax.shard_map(
        local,
        mesh=mesh,
        in_specs=(
            P("rep", ("col", "row")),
            P(),
            P("rep", ("row", "col")),
            P(("row", "col"), None, None),
            P(("row", "col")),
            P(("row", "col")),
            P(("row", "col")),
            P(("row", "col")),
        ),
        out_specs=(P("rep", ("row", "col")), P("rep", ("col", "row")), P("rep", None)),
        check_vma=False,
    )
```

profile of v0, /device:TPU:2, one launch (start us, length us, event | category | flops | bytes accessed | tf_op | source)
XLA Modules:
  0.0 1082.4 jit_solution(2901445615518222513)
XLA Ops:
  7.2 0.9 copy-done
  8.1 2.3 fusion.39
  10.5 0.0 all-gather.3.cloned.1.call-start
  10.5 30.2 %reduce-scatter.5.cloned.1.call-done = f32[64,512]{1,0:T(8,128)} async-done(((f32[256,512]{1,0:T(8,128)}), f32[64,512]{1,0:T(8,128)}) %reduce-scatter.5.cloned.1.call-update) | async-done | bytes 131088 | tf_op jit(solution)/shard_map/reduce_scatter | solution.py:46
  40.7 0.0 reduce-scatter.7.cloned.1.call-start
  41.4 0.7 compare_select_fusion.2
  42.1 14.2 %gather_fusion = f32[160,128,128]{2,1,0:T(8,128)} fusion(f32[160,128,128]{2,1,0:T(8,128)} %param.15, s32[1024]{0:T(1024)S(1)} %pad_clamp_fusion.2), kind=kCustom, calls=%fused_computation.clone | custom fusion | bytes 20972160 | tf_op jit(solution)/shard_map/jit(_take)/gather | solution.py:12
  56.3 10.5 all-gather.3.cloned.1.call-done
  66.8 1.3 copy_bitcast_fusion.3
  68.2 3.3 gather_fusion.1
  71.5 24.3 %fusion.20 = f32[64,160,128]{2,0,1:T(8,128)S(1)} fusion(f32[160,64,128]{2,1,0:T(8,128)} %gather_fusion.1, pred[160]{0:T(512)(128)(4,1)S(1)} %get-tuple-element.7, f32[160,128,128]{2,1,0:T(8,128)} %gather_fusion, pred[160]{0:T(512)(128)(4,1)S(1)} %get-tuple-element.8), kind=kOutput, calls=%fused_computation.23 | convolution fusion | flops 2017198080 | bytes 20971840 | tf_op jit(solution)/shard_map/fgb,gab->fga/dot_general | solution.py:16
  95.8 5.6 fusion.8
  101.5 1.6 copy.29
  103.1 0.0 all-gather.5.cloned.1.call-start
  103.1 87.2 %reduce-scatter.7.cloned.1.call-done = f32[64,512]{1,0:T(8,128)} async-done(((f32[64,4096]{1,0:T(8,128)}), f32[64,512]{1,0:T(8,128)}) %reduce-scatter.7.cloned.1.call-update) | async-done | bytes 131088 | tf_op jit(solution)/shard_map/reduce_scatter | solution.py:62
  190.4 1.7 fusion.36
  192.1 0.0 reduce-scatter.9.cloned.1.call-start
  192.2 59.1 %all-gather.5.cloned.1.call-done = f32[64,4096]{1,0:T(8,128)} async-done(((f32[64,512]{1,0:T(8,128)}), f32[64,4096]{1,0:T(8,128)}) %all-gather.5.cloned.1.call-update) | async-done | bytes 1048592 | tf_op jit(solution)/shard_map/all_gather | solution.py:65
  251.3 1.3 copy_bitcast_fusion.2
  252.7 3.3 gather_fusion.2
  255.9 13.9 %fusion.25 = f32[64,160,128]{2,0,1:T(8,128)S(1)} fusion(f32[160,64,128]{2,1,0:T(8,128)} %gather_fusion.2, pred[160]{0:T(512)(128)(4,1)S(1)} %compare_and_fusion, f32[160,128,128]{2,1,0:T(8,128)} %gather_fusion, pred[160]{0:T(512)(128)(4,1)S(1)} %get-tuple-element.8), kind=kOutput, calls=%fused_computation.24 | convolution fusion | flops 2017198080 | bytes 20971840 | tf_op jit(solution)/shard_map/fga,gab->fgb/dot_general | solution.py:14
  269.8 5.6 fusion.6
  275.5 1.6 copy.28
  277.1 0.0 all-reduce.2.cloned.1.call-start
  277.1 30.8 %reduce-scatter.9.cloned.1.call-done = f32[64,512]{1,0:T(8,128)} async-done(((f32[64,4096]{1,0:T(8,128)}), f32[64,512]{1,0:T(8,128)}) %reduce-scatter.9.cloned.1.call-update) | async-done | bytes 131088 | tf_op jit(solution)/shard_map/reduce_scatter | solution.py:69
  307.9 16.4 %all_gather.11 = f32[256,512]{1,0:T(8,128)S(1)} all-gather(f32[64,512]{1,0:T(8,128)} %reduce-scatter.9.cloned.1.call-done), channel_id=1, replica_groups=mesh['row'=8,'col'=8,'rep'=4] {'rep'}, dimensions={0}, use_global_device_ids=true | all-gather | bytes 655360 | tf_op jit(solution)/shard_map/all_gather | solution.py:83
  324.4 1.2 fusion.30
  325.6 0.0 reduce-scatter.11.cloned.1.call-start
  325.7 2.3 fusion.37
  328.0 722.2 %all-reduce.2.cloned.1.call-done = f32[64,256]{1,0:T(8,128)} async-done(((f32[64,256]{1,0:T(8,128)}), f32[64,256]{1,0:T(8,128)}) %all-reduce.2.cloned.1.call-update) | async-done | bytes 65552 | tf_op jit(solution)/shard_map/psum | solution.py:89
  1050.2 23.9 %reduce-scatter.11.cloned.1.call-done = f32[64,512]{1,0:T(8,128)} async-done(((f32[256,512]{1,0:T(8,128)}), f32[64,512]{1,0:T(8,128)}) %reduce-scatter.11.cloned.1.call-update) | async-done | bytes 131088 | tf_op jit(solution)/shard_map/reduce_scatter | solution.py:70
  1074.1 1.5 copy.32
  (27 shorter events, 0.2 us)
Async XLA Ops:
  7.2 1.0 copy-start
  7.2 33.5 %reduce-scatter.5.cloned.1.call-start = ((), (), s32[]{:S(2)}) async-start(), calls=%async_computation.4 | async-start | bytes 655360 | tf_op jit(solution)/shard_map/reduce_scatter | solution.py:46
  10.5 56.4 %all-gather.3.cloned.1.call-start = ((), (), s32[]{:S(2)}) async-start(), calls=%async_computation.5 | async-start | bytes 1179648 | tf_op jit(solution)/shard_map/all_gather | solution.py:58
  40.7 149.7 %reduce-scatter.7.cloned.1.call-start = ((), (), s32[]{:S(2)}) async-start(), calls=%async_computation.6 | async-start | bytes 1179648 | tf_op jit(solution)/shard_map/reduce_scatter | solution.py:62
  42.1 14.2 %copy-start.3 = (s32[160]{0:T(256)S(1)}, s32[160]{0:T(256)}, u32[]{:S(2)}) copy-start(s32[160]{0:T(256)} %param.17) | copy-start | bytes 1924
  42.1 14.2 %copy-start.5 = (s32[160]{0:T(256)S(1)}, s32[160]{0:T(256)}, u32[]{:S(2)}) copy-start(s32[160]{0:T(256)} %param.18) | copy-start | bytes 1924
  71.5 24.3 %copy-start.4 = (s32[160]{0:T(256)S(1)}, s32[160]{0:T(256)}, u32[]{:S(2)}) copy-start(s32[160]{0:T(256)} %param.16) | copy-start | bytes 1924
  95.8 94.6 %copy-start.2 = (f32[64,512]{1,0:T(8,128)S(1)}, f32[64,512]{1,0:T(8,128)}, u32[]{:S(2)}) copy-start(f32[64,512]{1,0:T(8,128)} %param.14) | copy-start | bytes 393220
  103.1 148.2 %all-gather.5.cloned.1.call-start = ((), (), s32[]{:S(2)}) async-start(), calls=%async_computation.7 | async-start | bytes 1179648 | tf_op jit(solution)/shard_map/all_gather | solution.py:65
  192.1 115.8 %reduce-scatter.9.cloned.1.call-start = ((), (), s32[]{:S(2)}) async-start(), calls=%async_computation.8 | async-start | bytes 1179648 | tf_op jit(solution)/shard_map/reduce_scatter | solution.py:69
  269.8 54.5 %copy-start.1 = (f32[64,512]{1,0:T(8,128)S(1)}, f32[64,512]{1,0:T(8,128)}, u32[]{:S(2)}) copy-start(f32[64,512]{1,0:T(8,128)} %param.12) | copy-start | bytes 393220
  277.1 773.1 %all-reduce.2.cloned.1.call-start = ((), (), s32[]{:S(2)}) async-start(), calls=%async_computation.10 | async-start | bytes 131072 | tf_op jit(solution)/shard_map/psum | solution.py:89
  325.6 748.5 %reduce-scatter.11.cloned.1.call-start = ((), (), s32[]{:S(2)}) async-start(), calls=%async_computation.9 | async-start | bytes 655360 | tf_op jit(solution)/shard_map/reduce_scatter | solution.py:70
Sparse Core Ops, SparseCore 0:
  10.6 30.0 reduce-scatter.4
  42.5 24.2 all-gather.2
  103.2 87.1 reduce-scatter.6
  193.4 57.8 all-gather.4
  277.2 30.6 reduce-scatter.8
  325.7 724.4 all-reduce.1
  1053.3 20.7 reduce-scatter.10
where the time goes:
time: 1080 us
  waiting for transfers between devices  964 us (89%)
  matrix products  55.3 us (5%)
  local copies, waits for them, and re-layouts  29 us (3%)
  blocking collectives  16.4 us (2%)
  between operations  14.9 us (1%)
    psum x1, waiting for transfers between devices, local(): lax.psum(weight_part * float(node_total) ** (-0.5), ('row', 'col'))  722 us
    reduce_scatter x1, waiting for transfers between devices, local(): lax.psum_scatter(partial_value, 'col', scatter_dimension=1, tiled=True)  87.2 us
    all_gather x1, waiting for transfers between devices, local(): row_block = lax.all_gather(grad_pre, 'col', axis=1, tiled=True)  59.1 us
    reduce_scatter x1, waiting for transfers between devices, local(): lax.psum_scatter(partial_back, 'row', scatter_dimension=1, tiled=True)  30.8 us
    reduce_scatter x1, waiting for transfers between devices, local(): lax.psum_scatter(lax.dot_general(own_rows, features, (((0,), (0,)), ((),...  30.2 us
    dot_general x1, matrix products, tile_terms(): jnp.einsum('fgb,gab->fga', picked, chosen, precision=lax.Precision.HIGHEST)  24.3 us
    reduce_scatter x1, waiting for transfers between devices, local(): lax.psum_scatter(jnp.dot(own_cols, grad_mixed, preferred_element_type=jnp...  23.9 us
  transfers between devices with their start and end apart: 7, of which 7 were waited for; matrix products, arithmetic and copies ran while one was open for 2% of the time, Pallas kernels for 0%

commit v1 on v0

--- a/solution.py
+++ b/solution.py
@@ -86,7 +86,9 @@
         preferred_element_type=jnp.float32,
     )
     node_total = stretch_len * n_rowdev * n_coldev
-    weight_grad = lax.psum(weight_part * float(node_total) ** (-0.5), ("row", "col"))
+    weight_grad = jnp.sum(
+        lax.all_gather(weight_part * float(node_total) ** (-0.5), ("row", "col")), axis=0
+    )
     return (output, input_grad, weight_grad)
 
 

time: 1080 us -> 447 us (0.41)
  waiting for transfers between devices: 964 us -> 327 us
    psum x1 -> x0, waiting for transfers between devices: 722 us -> none  [local(): lax.psum(weight_part * float(node_total) ** (-0.5), ('row', 'col'))]
    all_gather x0 -> x1, waiting for transfers between devices: none -> 86.8 us  [local(): lax.all_gather(weight_part * float(node_total) ** (-0.5), ('row', 'col'))]
  transfers between devices with their start and end apart: 7 -> 7, of which waited for: 7 -> 7; matrix products, arithmetic and copies ran while one was open for 2% -> 5% of each run, Pallas kernels for 0% -> 0%
where the time goes in v1:
time: 447 us
  waiting for transfers between devices  327 us (73%)
  matrix products  55.4 us (12%)
  local copies, waits for them, and re-layouts  27.5 us (6%)
  blocking collectives  16.4 us (4%)
  between operations  14.9 us (3%)
  other arithmetic  5.49 us (1%)
    reduce_scatter x1, waiting for transfers between devices, local(): lax.psum_scatter(partial_value, 'col', scatter_dimension=1, tiled=True)  87.2 us
    all_gather x1, waiting for transfers between devices, local(): lax.all_gather(weight_part * float(node_total) ** (-0.5), ('row', 'col'))  86.8 us
    all_gather x1, waiting for transfers between devices, local(): row_block = lax.all_gather(grad_pre, 'col', axis=1, tiled=True)  59.1 us
    reduce_scatter x1, waiting for transfers between devices, local(): lax.psum_scatter(partial_back, 'row', scatter_dimension=1, tiled=True)  30.8 us
    reduce_scatter x1, waiting for transfers between devices, local(): lax.psum_scatter(lax.dot_general(own_rows, features, (((0,), (0,)), ((),...  30.2 us
    dot_general x1, matrix products, tile_terms(): jnp.einsum('fgb,gab->fga', picked, chosen, precision=lax.Precision.HIGHEST)  24.3 us
    reduce_scatter x1, waiting for transfers between devices, local(): lax.psum_scatter(jnp.dot(own_cols, grad_mixed, preferred_element_type=jnp...  22.3 us
    all_gather x1, blocking collectives, local(): lax.all_gather(grad_mixed, 'rep', axis=0, tiled=True)  16.4 us
  transfers between devices with their start and end apart: 7, of which 7 were waited for; matrix products, arithmetic and copies ran while one was open for 5% of the time, Pallas kernels for 0%

profile of v1, /device:TPU:2, one launch (start us, length us, event | category | flops | bytes accessed | tf_op | source)
XLA Modules:
  0.0 447.0 jit_solution(1629889419929185207)
XLA Ops:
  7.2 0.9 copy-done
  8.1 2.3 fusion.39
  10.5 0.0 all-gather.5.cloned.1.call-start
  10.5 30.2 %reduce-scatter.5.cloned.1.call-done = f32[64,512]{1,0:T(8,128)} async-done(((f32[256,512]{1,0:T(8,128)}), f32[64,512]{1,0:T(8,128)}) %reduce-scatter.5.cloned.1.call-update) | async-done | bytes 131088 | tf_op jit(solution)/shard_map/reduce_scatter | solution.py:46
  40.7 0.0 reduce-scatter.7.cloned.1.call-start
  41.4 0.7 compare_select_fusion.2
  42.1 14.2 %gather_fusion = f32[160,128,128]{2,1,0:T(8,128)} fusion(f32[160,128,128]{2,1,0:T(8,128)} %param.15, s32[1024]{0:T(1024)S(1)} %pad_clamp_fusion.2), kind=kCustom, calls=%fused_computation.clone | custom fusion | bytes 20972160 | tf_op jit(solution)/shard_map/jit(_take)/gather | solution.py:12
  56.3 10.5 %all-gather.5.cloned.1.call-done = f32[64,4096]{1,0:T(8,128)} async-done(((f32[64,512]{1,0:T(8,128)}), f32[64,4096]{1,0:T(8,128)}) %all-gather.5.cloned.1.call-update) | async-done | bytes 1048592 | tf_op jit(solution)/shard_map/all_gather | solution.py:58
  66.8 1.3 copy_bitcast_fusion.3
  68.2 3.3 gather_fusion.1
  71.5 24.3 %fusion.20 = f32[64,160,128]{2,0,1:T(8,128)S(1)} fusion(f32[160,64,128]{2,1,0:T(8,128)} %gather_fusion.1, pred[160]{0:T(512)(128)(4,1)S(1)} %get-tuple-element.7, f32[160,128,128]{2,1,0:T(8,128)} %gather_fusion, pred[160]{0:T(512)(128)(4,1)S(1)} %get-tuple-element.8), kind=kOutput, calls=%fused_computation.23 | convolution fusion | flops 2017198080 | bytes 20971840 | tf_op jit(solution)/shard_map/fgb,gab->fga/dot_general | solution.py:16
  95.8 5.6 %fusion.8 = f32[32,64,128]{2,0,1:T(8,128)S(1)} fusion(f32[64,160,128]{2,0,1:T(8,128)S(1)} %fusion.20, f32[160]{0:T(256)S(1)} %compare_convert_fusion, s32[160]{0:T(256)S(1)} %copy-done.4), kind=kOutput, calls=%fused_computation.11 | convolution fusion | flops 503326720 | bytes 6292736 | tf_op jit(solution)/shard_map/fgt,gd->fdt/dot_general | solution.py:21
  101.5 1.6 copy.29
  103.1 0.0 all-gather.7.cloned.1.call-start
  103.1 87.2 %reduce-scatter.7.cloned.1.call-done = f32[64,512]{1,0:T(8,128)} async-done(((f32[64,4096]{1,0:T(8,128)}), f32[64,512]{1,0:T(8,128)}) %reduce-scatter.7.cloned.1.call-update) | async-done | bytes 131088 | tf_op jit(solution)/shard_map/reduce_scatter | solution.py:62
  190.4 1.7 fusion.36
  192.1 0.0 reduce-scatter.9.cloned.1.call-start
  192.2 59.1 %all-gather.7.cloned.1.call-done = f32[64,4096]{1,0:T(8,128)} async-done(((f32[64,512]{1,0:T(8,128)}), f32[64,4096]{1,0:T(8,128)}) %all-gather.7.cloned.1.call-update) | async-done | bytes 1048592 | tf_op jit(solution)/shard_map/all_gather | solution.py:65
  251.3 1.3 copy_bitcast_fusion.2
  252.7 3.3 gather_fusion.2
  255.9 13.9 %fusion.25 = f32[64,160,128]{2,0,1:T(8,128)S(1)} fusion(f32[160,64,128]{2,1,0:T(8,128)} %gather_fusion.2, pred[160]{0:T(512)(128)(4,1)S(1)} %compare_and_fusion, f32[160,128,128]{2,1,0:T(8,128)} %gather_fusion, pred[160]{0:T(512)(128)(4,1)S(1)} %get-tuple-element.8), kind=kOutput, calls=%fused_computation.24 | convolution fusion | flops 2017198080 | bytes 20971840 | tf_op jit(solution)/shard_map/fga,gab->fgb/dot_general | solution.py:14
  269.8 5.6 %fusion.6 = f32[32,64,128]{2,0,1:T(8,128)S(1)} fusion(f32[64,160,128]{2,0,1:T(8,128)S(1)} %fusion.25, s32[160]{0:T(256)S(1)} %copy-done.3, f32[160]{0:T(256)S(1)} %compare_convert_fusion), kind=kOutput, calls=%fused_computation.9 | convolution fusion | flops 503326720 | bytes 6292736 | tf_op jit(solution)/shard_map/fgt,gd->fdt/dot_general | solution.py:21
  275.5 1.6 copy.28
  277.1 0.0 all-gather.9.cloned.1.call-start
  277.1 30.8 %reduce-scatter.9.cloned.1.call-done = f32[64,512]{1,0:T(8,128)} async-done(((f32[64,4096]{1,0:T(8,128)}), f32[64,512]{1,0:T(8,128)}) %reduce-scatter.9.cloned.1.call-update) | async-done | bytes 131088 | tf_op jit(solution)/shard_map/reduce_scatter | solution.py:69
  307.9 16.4 %all_gather.17 = f32[256,512]{1,0:T(8,128)S(1)} all-gather(f32[64,512]{1,0:T(8,128)} %reduce-scatter.9.cloned.1.call-done), channel_id=1, replica_groups=mesh['row'=8,'col'=8,'rep'=4] {'rep'}, dimensions={0}, use_global_device_ids=true | all-gather | bytes 655360 | tf_op jit(solution)/shard_map/all_gather | solution.py:83
  324.4 1.2 fusion.30
  325.6 0.0 reduce-scatter.11.cloned.1.call-start
  325.7 2.3 fusion.37
  328.0 86.8 %all-gather.9.cloned.1.call-done = f32[4096,256]{1,0:T(8,128)} async-done(((f32[64,256]{1,0:T(8,128)}), f32[4096,256]{1,0:T(8,128)}) %all-gather.9.cloned.1.call-update) | async-done | bytes 4194320 | tf_op jit(solution)/shard_map/all_gather | solution.py:90
  414.8 3.1 reduce_sum.9
  417.9 22.3 %reduce-scatter.11.cloned.1.call-done = f32[64,512]{1,0:T(8,128)} async-done(((f32[256,512]{1,0:T(8,128)}), f32[64,512]{1,0:T(8,128)}) %reduce-scatter.11.cloned.1.call-update) | async-done | bytes 131088 | tf_op jit(solution)/shard_map/reduce_scatter | solution.py:70
  (27 shorter events, 0.2 us)
Async XLA Ops:
  7.2 1.0 copy-start
  7.2 33.5 %reduce-scatter.5.cloned.1.call-start = ((), (), s32[]{:S(2)}) async-start(), calls=%async_computation.4 | async-start | bytes 655360 | tf_op jit(solution)/shard_map/reduce_scatter | solution.py:46
  10.5 56.4 %all-gather.5.cloned.1.call-start = ((), (), s32[]{:S(2)}) async-start(), calls=%async_computation.5 | async-start | bytes 1179648 | tf_op jit(solution)/shard_map/all_gather | solution.py:58
  40.7 149.7 %reduce-scatter.7.cloned.1.call-start = ((), (), s32[]{:S(2)}) async-start(), calls=%async_computation.6 | async-start | bytes 1179648 | tf_op jit(solution)/shard_map/reduce_scatter | solution.py:62
  42.1 14.2 %copy-start.3 = (s32[160]{0:T(256)S(1)}, s32[160]{0:T(256)}, u32[]{:S(2)}) copy-start(s32[160]{0:T(256)} %param.17) | copy-start | bytes 1924
  42.1 14.2 %copy-start.5 = (s32[160]{0:T(256)S(1)}, s32[160]{0:T(256)}, u32[]{:S(2)}) copy-start(s32[160]{0:T(256)} %param.18) | copy-start | bytes 1924
  71.5 24.3 %copy-start.4 = (s32[160]{0:T(256)S(1)}, s32[160]{0:T(256)}, u32[]{:S(2)}) copy-start(s32[160]{0:T(256)} %param.16) | copy-start | bytes 1924
  95.8 94.6 %copy-start.2 = (f32[64,512]{1,0:T(8,128)S(1)}, f32[64,512]{1,0:T(8,128)}, u32[]{:S(2)}) copy-start(f32[64,512]{1,0:T(8,128)} %param.14) | copy-start | bytes 393220
  103.1 148.2 %all-gather.7.cloned.1.call-start = ((), (), s32[]{:S(2)}) async-start(), calls=%async_computation.7 | async-start | bytes 1179648 | tf_op jit(solution)/shard_map/all_gather | solution.py:65
  192.1 115.8 %reduce-scatter.9.cloned.1.call-start = ((), (), s32[]{:S(2)}) async-start(), calls=%async_computation.8 | async-start | bytes 1179648 | tf_op jit(solution)/shard_map/reduce_scatter | solution.py:69
  269.8 54.5 %copy-start.1 = (f32[64,512]{1,0:T(8,128)S(1)}, f32[64,512]{1,0:T(8,128)}, u32[]{:S(2)}) copy-start(f32[64,512]{1,0:T(8,128)} %param.12) | copy-start | bytes 393220
  277.1 137.7 %all-gather.9.cloned.1.call-start = ((), (), s32[]{:S(2)}) async-start(), calls=%async_computation.10 | async-start | bytes 4259840 | tf_op jit(solution)/shard_map/all_gather | solution.py:90
  325.6 114.5 %reduce-scatter.11.cloned.1.call-start = ((), (), s32[]{:S(2)}) async-start(), calls=%async_computation.9 | async-start | bytes 655360 | tf_op jit(solution)/shard_map/reduce_scatter | solution.py:70
Sparse Core Ops, SparseCore 0:
  10.6 30.0 reduce-scatter.4
  42.5 24.2 all-gather.4
  103.2 87.1 reduce-scatter.6
  193.4 57.8 all-gather.6
  277.2 30.6 reduce-scatter.8
  325.7 89.0 all-gather.8
  417.9 22.1 reduce-scatter.10
